TPU v7x, 512 devices: a whole 4x8x8 slice. The times are simulated.
512 devices in a mesh: docs: 128 (over y, z, core), split: 4 (over x).
Axes of the slice: x: 4, y: 8, z: 8, core: 2. Of those that a mesh axis runs over, the one named last changes fastest.
Arguments:
- embeddings: bfloat16 [65536, 1024], P(('docs', 'split')), may hold values from -480 to 480
- cluster_id: int32 [65536], P(('docs', 'split')), may hold values from 0 to 255, as said below
- rank: int32 [65536], P(('docs', 'split')), may hold values from 0 to 65535, each once
Outputs:
- dup_score: float32 [65536], P(('docs', 'split'))
Inputs may be any that keep to these rules, and one draw needn't show every extreme that they name: `cluster_id`: cluster c belongs to owner c // 2. In each aligned block of 128 documents (the documents of one device) at most 2 documents belong to any one owner, and one owner receives exactly 2 from every block.
All inputs are finite; a program needn't handle non-finite values.
Results may differ from a plain program's by a relative error of at most 0.00056.
Values may be sent and summed in bfloat16 or wider, within the bound.
No kernel may reach another device: no remote copies, remote signals or barrier semaphores. Data moves between devices by JAX's collectives and lax.ppermute only.
A program may use at most 64 MiB of HBM per device.

v0:
```python
import jax
import jax.numpy as jnp
from jax import lax
from jax.sharding import PartitionSpec as P

D = 1024
CL_DEV = 2
EPSILON = 1e-06


def per_device(embeddings, cluster_id, rank):
    values = embeddings.astype(jnp.float32)
    unit = (values / jnp.sqrt(jnp.sum(values * values, axis=1, keepdims=True) + EPSILON)).astype(
        jnp.bfloat16
    )
    owners = lax.axis_size("docs")
    local_docs = embeddings.shape[0]
    capacity = 2 * local_docs // owners
    slots_all = owners * capacity
    owner = cluster_id // CL_DEV
    onehot = (owner[:, None] == jnp.arange(owners, dtype=jnp.int32)[None, :]).astype(jnp.int32)
    before = jnp.cumsum(onehot, axis=0) - onehot
    slot_index = jnp.sum(before * onehot, axis=1)
    target = owner * capacity + slot_index
    send_rows = jnp.zeros((slots_all, D), jnp.bfloat16).at[target].set(unit)
    send_cluster = jnp.full((slots_all,), -1, jnp.int32).at[target].set(cluster_id)
    send_rank = jnp.zeros((slots_all,), jnp.int32).at[target].set(rank)
    got_rows, got_cluster, got_rank = (
        lax.all_to_all(
            send_rows.reshape(owners, capacity, D), "docs", split_axis=0, concat_axis=0, tiled=True
        ),
        lax.all_to_all(
            send_cluster.reshape(owners, capacity), "docs", split_axis=0, concat_axis=0, tiled=True
        ),
        lax.all_to_all(
            send_rank.reshape(owners, capacity), "docs", split_axis=0, concat_axis=0, tiled=True
        ),
    )
    queries = got_rows.reshape(slots_all, D)
    query_cluster = got_cluster.reshape(slots_all)
    query_rank = got_rank.reshape(slots_all)

    def pair_scores(rows_other):
        return jnp.einsum("qd,kd->qk", queries, rows_other, preferred_element_type=jnp.float32)

    def row_best(rows_other, cluster_other, rank_other):
        scores = pair_scores(rows_other)
        allowed = (query_cluster[:, None] == cluster_other[None, :]) & (
            rank_other[None, :] < query_rank[:, None]
        )
        return jnp.max(jnp.where(allowed, scores, -1.0), axis=1)

    start_best = jnp.full((slots_all,), -1.0, jnp.float32)
    rows_piece = lax.all_gather(queries, "split", axis=0, tiled=True)
    cluster_piece = lax.all_gather(query_cluster, "split", axis=0, tiled=True)
    rank_piece = lax.all_gather(query_rank, "split", axis=0, tiled=True)
    total = rows_piece.shape[0]
    pieces = total // slots_all
    stacked = (
        rows_piece.reshape(pieces, slots_all, D),
        cluster_piece.reshape(pieces, slots_all),
        rank_piece.reshape(pieces, slots_all),
    )

    def advance(top_score, member):
        return (jnp.maximum(top_score, row_best(member[0], member[1], member[2])), None)

    result, _ = lax.scan(advance, start_best, stacked)
    top_score = result
    returned_scores = lax.all_to_all(
        top_score.reshape(owners, capacity), "docs", split_axis=0, concat_axis=0, tiled=True
    )
    return returned_scores.reshape(slots_all)[target]


def solution(mesh):
    placed = (P(("docs", "split"), None), P(("docs", "split")), P(("docs", "split")))
    return jax.shard_map(
        per_device, mesh=mesh, in_specs=placed, out_specs=P(("docs", "split")), check_vma=False
    )
```

profile of v0, /device:TPU:1, one launch (start us, length us, event | category | flops | bytes accessed | tf_op | source)
XLA Modules:
  0.0 138.9 jit_solution(11490728331037051452)
XLA Ops:
  6.5 0.0 all-gather.4.cloned.1.call-start
  6.5 0.7 and_select_fusion
  7.2 0.1 fusion.11
  7.3 0.2 reduce_window_sum.11
  7.5 0.2 select_reduce_fusion
  7.6 0.7 compare_select_fusion
  8.3 1.1 fusion.5
  9.4 1.8 %scatter_custom_fusion.2 = bf16[256,1024]{1,0:T(8,128)(2,1)S(1)} fusion(s32[128]{0:T(128)S(1)} %compare_select_fusion, bf16[128,1024]{1,0:T(8,128)(2,1)} %param.5, f32[128]{0:T(128)S(1)} %add_sqrt_fusion, bf16[]{:T(256)} %constant.41.clone.1), kind=kCustom, calls=%fused_computation.17 | custom fusion | flops 393216 | bytes 786946 | tf_op jit(solution)/shard_map/scatter | solution.py:25
  11.2 0.2 reshape.52
  11.4 37.6 %all_to_all.38 = bf16[128,2,1024]{2,1,0:T(2,128)(2,1)S(1)} all-to-all(bf16[128,2,1024]{2,1,0:T(2,128)(2,1)S(1)} %reshape.52), channel_id=1, replica_groups=mesh['docs'=128,'split'=4] {'docs'}, dimensions={0} | all-to-all | bytes 1048576 | tf_op jit(solution)/shard_map/all_to_all | solution.py:29
  49.1 1.0 reshape.53
  50.1 0.0 all-gather.4.cloned.1.call-update
  50.1 1.1 scatter_custom_fusion.1
  51.2 0.8 all_to_all.28
  51.9 7.2 %all-to-all-start.1 = ((s32[128,1,2]{2,1,0:T(1,128)}), s32[128,1,2]{2,1,0:T(1,128)S(1)}, u32[]{:S(2)}, u32[]{:S(2)}) async-start(s32[128,1,2]{2,1,0:T(1,128)} %bitcast.2), calls=%async_computation.1 | async-start | bytes 131072 | tf_op jit(solution)/shard_map/all_to_all | solution.py:35
  59.1 1.1 scatter_custom_fusion
  60.2 0.8 all_to_all.25
  61.0 9.8 %all-to-all-done.1 = s32[128,1,2]{2,1,0:T(1,128)S(1)} async-done(((s32[128,1,2]{2,1,0:T(1,128)}), s32[128,1,2]{2,1,0:T(1,128)S(1)}, u32[]{:S(2)}, u32[]{:S(2)}) %all-to-all-start.1) | async-done | bytes 1056 | tf_op jit(solution)/shard_map/all_to_all | solution.py:35
  70.8 0.0 copy-start
  70.8 5.7 %all-to-all-start = ((s32[128,1,2]{2,1,0:T(1,128)}), s32[128,1,2]{2,1,0:T(1,128)S(1)}, u32[]{:S(2)}, u32[]{:S(2)}) async-start(s32[128,1,2]{2,1,0:T(1,128)} %bitcast), calls=%async_computation | async-start | bytes 131072 | tf_op jit(solution)/shard_map/all_to_all | solution.py:32
  76.6 0.6 broadcast.46
  77.1 0.8 reduce.10
  78.0 0.1 reshape.94
  78.1 7.7 %all-gather.1 = s32[4,1,256]{2,1,0:T(1,128)S(1)} all-gather(s32[1,1,256]{2,1,0:T(1,128)S(1)} %reshape.94), channel_id=1, replica_groups=mesh['docs'=128,'split'=4] {'split'}, dimensions={0}, use_global_device_ids=true | all-gather | bytes 5120 | tf_op jit(solution)/shard_map/all_gather | solution.py:56
  85.8 2.4 %all-to-all-done = s32[128,1,2]{2,1,0:T(1,128)S(1)} async-done(((s32[128,1,2]{2,1,0:T(1,128)}), s32[128,1,2]{2,1,0:T(1,128)S(1)}, u32[]{:S(2)}, u32[]{:S(2)}) %all-to-all-start) | async-done | bytes 1056 | tf_op jit(solution)/shard_map/all_to_all | solution.py:32
  88.2 0.0 copy-start.1
  88.2 0.8 reduce.9
  89.1 0.1 reshape.92
  89.2 7.7 %all-gather = s32[4,1,256]{2,1,0:T(1,128)S(1)} all-gather(s32[1,1,256]{2,1,0:T(1,128)S(1)} %reshape.92), channel_id=1, replica_groups=mesh['docs'=128,'split'=4] {'split'}, dimensions={0}, use_global_device_ids=true | all-gather | bytes 5120 | tf_op jit(solution)/shard_map/all_gather | solution.py:55
  96.9 0.1 eq.59
  97.1 0.1 lt.37
  97.2 0.0 all-gather.4.cloned.1.call-done
  97.2 0.0 copy-done
  97.2 0.0 copy-done.1
  97.3 6.5 %while.12 = (s32[]{:T(128)}, f32[256]{0:T(256)S(1)}, s32[128,2]{1,0:T(8,128)}, s32[4,256]{1,0:T(4,128)S(1)}, s32[4,256]{1,0:T(4,128)S(1)}, /*index=5*/s32[128,2]...) while((s32[]{:T(128)}, f32[256]{0:T(256)S(1)}, ...), condition=%wide.wide.region_8.9_spmd.clone, body=%wide.wide.region_6.8_spmd.clone.sunk | while | flops 134545664 | bytes 1061507 | solution.py:68
  97.3 1.6 %fusion.25 = f32[256]{0:T(256)S(1)} fusion(bf16[256,1024]{1,0:T(8,128)(2,1)} %get-tuple-element.222, bf16[4,256,1024]{2,1,0:T(8,128)(2,1)} %get-tuple-element.221, s32[]{:T(128)} %get-tuple-element.203, s32[256]{0:T(256)S(1)} %get-tuple-element.223, s32[256]{0:T(256)S(1)} %get-tuple-element.224, s32[256]{0:T(256)S(1)} %bitcast.43, ...), kind=kOutput, calls=%fused_computation.6.clone.clone.1 | convolution fusion | flops 134545152 | bytes 1054208 | tf_op jit(solution)/shard_map/while/body/eval_jaxpr/qd,kd->qk/dot_general | solution.py:44
  98.9 1.6 %fusion.25 = f32[256]{0:T(256)S(1)} fusion(bf16[256,1024]{1,0:T(8,128)(2,1)} %get-tuple-element.222, bf16[4,256,1024]{2,1,0:T(8,128)(2,1)} %get-tuple-element.221, s32[]{:T(128)} %get-tuple-element.203, s32[256]{0:T(256)S(1)} %get-tuple-element.223, s32[256]{0:T(256)S(1)} %get-tuple-element.224, s32[256]{0:T(256)S(1)} %bitcast.43, ...), kind=kOutput, calls=%fused_computation.6.clone.clone.1 | convolution fusion | flops 134545152 | bytes 1054208 | tf_op jit(solution)/shard_map/while/body/eval_jaxpr/qd,kd->qk/dot_general | solution.py:44
  100.5 1.6 %fusion.25 = f32[256]{0:T(256)S(1)} fusion(bf16[256,1024]{1,0:T(8,128)(2,1)} %get-tuple-element.222, bf16[4,256,1024]{2,1,0:T(8,128)(2,1)} %get-tuple-element.221, s32[]{:T(128)} %get-tuple-element.203, s32[256]{0:T(256)S(1)} %get-tuple-element.223, s32[256]{0:T(256)S(1)} %get-tuple-element.224, s32[256]{0:T(256)S(1)} %bitcast.43, ...), kind=kOutput, calls=%fused_computation.6.clone.clone.1 | convolution fusion | flops 134545152 | bytes 1054208 | tf_op jit(solution)/shard_map/while/body/eval_jaxpr/qd,kd->qk/dot_general | solution.py:44
  102.1 1.6 %fusion.25 = f32[256]{0:T(256)S(1)} fusion(bf16[256,1024]{1,0:T(8,128)(2,1)} %get-tuple-element.222, bf16[4,256,1024]{2,1,0:T(8,128)(2,1)} %get-tuple-element.221, s32[]{:T(128)} %get-tuple-element.203, s32[256]{0:T(256)S(1)} %get-tuple-element.223, s32[256]{0:T(256)S(1)} %get-tuple-element.224, s32[256]{0:T(256)S(1)} %bitcast.43, ...), kind=kOutput, calls=%fused_computation.6.clone.clone.1 | convolution fusion | flops 134545152 | bytes 1054208 | tf_op jit(solution)/shard_map/while/body/eval_jaxpr/qd,kd->qk/dot_general | solution.py:44
  103.7 0.8 all_to_all.32
  104.5 12.7 %all-to-all-start.3 = ((f32[128,1,2]{2,1,0:T(1,128)}), f32[128,1,2]{2,1,0:T(1,128)S(1)}, u32[]{:S(2)}, u32[]{:S(2)}) async-start(f32[128,1,2]{2,1,0:T(1,128)} %bitcast.5), calls=%async_computation.3 | async-start | bytes 131072 | tf_op jit(solution)/shard_map/all_to_all | solution.py:70
  117.2 11.6 %all-to-all-done.3 = f32[128,1,2]{2,1,0:T(1,128)S(1)} async-done(((f32[128,1,2]{2,1,0:T(1,128)}), f32[128,1,2]{2,1,0:T(1,128)S(1)}, u32[]{:S(2)}, u32[]{:S(2)}) %all-to-all-start.3) | async-done | bytes 1056 | tf_op jit(solution)/shard_map/all_to_all | solution.py:70
  128.8 0.5 broadcast.48
  129.3 0.8 reduce.11
  130.1 0.1 reshape.55
  130.3 1.8 %gather_fusion = f32[128]{0:T(128)} fusion(f32[256]{0:T(256)S(1)} %reshape.55, s32[1024]{0:T(1024)S(1)} %pad_clamp_fusion), kind=kCustom, calls=%fused_computation | custom fusion | bytes 1536 | tf_op jit(solution)/shard_map/gather | solution.py:73
  (13 shorter events, 0.1 us)
Async XLA Ops:
  6.5 90.7 %all-gather.4.cloned.1.call-start = ((), (), s32[]{:S(2)}) async-start(), calls=%async_computation.4 | async-start | bytes 2621440 | tf_op jit(solution)/shard_map/all_gather | solution.py:54
  51.9 18.9 %all-to-all-start.1 = ((s32[128,1,2]{2,1,0:T(1,128)}), s32[128,1,2]{2,1,0:T(1,128)S(1)}, u32[]{:S(2)}, u32[]{:S(2)}) async-start(s32[128,1,2]{2,1,0:T(1,128)} %bitcast.2), calls=%async_computation.1 | async-start | bytes 131072 | tf_op jit(solution)/shard_map/all_to_all | solution.py:35
  70.8 26.4 %copy-start = (s32[128,1,2]{2,1,0:T(1,128)}, s32[128,1,2]{2,1,0:T(1,128)S(1)}, u32[]{:S(2)}) copy-start(s32[128,1,2]{2,1,0:T(1,128)S(1)} %all-to-all-done.1) | copy-start | bytes 3076
  70.8 17.4 %all-to-all-start = ((s32[128,1,2]{2,1,0:T(1,128)}), s32[128,1,2]{2,1,0:T(1,128)S(1)}, u32[]{:S(2)}, u32[]{:S(2)}) async-start(s32[128,1,2]{2,1,0:T(1,128)} %bitcast), calls=%async_computation | async-start | bytes 131072 | tf_op jit(solution)/shard_map/all_to_all | solution.py:32
  88.2 9.0 %copy-start.1 = (s32[128,1,2]{2,1,0:T(1,128)}, s32[128,1,2]{2,1,0:T(1,128)S(1)}, u32[]{:S(2)}) copy-start(s32[128,1,2]{2,1,0:T(1,128)S(1)} %all-to-all-done) | copy-start | bytes 3076
  104.5 24.3 %all-to-all-start.3 = ((f32[128,1,2]{2,1,0:T(1,128)}), f32[128,1,2]{2,1,0:T(1,128)S(1)}, u32[]{:S(2)}, u32[]{:S(2)}) async-start(f32[128,1,2]{2,1,0:T(1,128)} %bitcast.5), calls=%async_computation.3 | async-start | bytes 131072 | tf_op jit(solution)/shard_map/all_to_all | solution.py:70
Sparse Core Ops, SparseCore 0:
  50.2 29.5 all-gather.3
where the time goes:
time: 139 us
  blocking collectives  53.1 us (38%)
  starting transfers between devices  25.6 us (18%)
  waiting for transfers between devices  23.8 us (17%)
  between operations  13.6 us (10%)
  local copies, waits for them, and re-layouts  9.27 us (7%)
  other arithmetic  7.19 us (5%)
  matrix products  6.24 us (4%)
    all_to_all x1, blocking collectives, per_device(): lax.all_to_all(send_rows.reshape(owners, capacity, D), 'docs', split_axis...  37.6 us
    all_to_all x1, starting transfers between devices, per_device(): lax.all_to_all(top_score.reshape(owners, capacity), 'docs', split_axis=0,...  12.7 us
    all_to_all x1, waiting for transfers between devices, per_device(): lax.all_to_all(top_score.reshape(owners, capacity), 'docs', split_axis=0,...  11.6 us
    all_to_all x1, waiting for transfers between devices, per_device(): lax.all_to_all(send_rank.reshape(owners, capacity), 'docs', split_axis=0,...  9.83 us
    all_gather x1, blocking collectives, per_device(): cluster_piece = lax.all_gather(query_cluster, 'split', axis=0, tiled=True)  7.72 us
    all_gather x1, blocking collectives, per_device(): rank_piece = lax.all_gather(query_rank, 'split', axis=0, tiled=True)  7.71 us
    all_to_all x1, starting transfers between devices, per_device(): lax.all_to_all(send_rank.reshape(owners, capacity), 'docs', split_axis=0,...  7.17 us
    dot_general x4, matrix products, pair_scores(): jnp.einsum('qd,kd->qk', queries, rows_other, preferred_element_type=jnp.f...  6.24 us
  transfers between devices with their start and end apart: 4, of which 3 were waited for; matrix products, arithmetic and copies ran while one was open for 4% of the time, Pallas kernels for 0%

commit v1 on v0

--- a/solution.py
+++ b/solution.py
@@ -52,7 +52,12 @@
 
     start_best = jnp.full((slots_all,), -1.0, jnp.float32)
     rows_piece = lax.all_gather(queries, "split", axis=0, tiled=True)
-    cluster_piece = lax.all_gather(query_cluster, "split", axis=0, tiled=True)
+    cluster_piece = jnp.concatenate(
+        lax.all_to_all(
+            jnp.stack([query_cluster for _ in range(lax.psum(1, "split"))], 0), "split", 0, 0
+        ),
+        0,
+    )
     rank_piece = lax.all_gather(query_rank, "split", axis=0, tiled=True)
     total = rows_piece.shape[0]
     pieces = total // slots_all

time: 139 us -> 140 us (level)
  waiting for transfers between devices: 23.8 us -> 31.8 us
  blocking collectives: 53.1 us -> 45.5 us
    all_gather x1 -> x0, blocking collectives: 7.72 us -> none  [per_device(): cluster_piece = lax.all_gather(query_cluster, 'split', axis=0, tiled=True)]
    all_to_all x1, waiting for transfers between devices: 2.39 us -> 9.83 us  [per_device(): lax.all_to_all(send_cluster.reshape(owners, capacity), 'docs', split_axis...]
    all_to_all x1, starting transfers between devices: 12.7 us -> 8.29 us  [per_device(): lax.all_to_all(top_score.reshape(owners, capacity), 'docs', split_axis=0,...]
    all_to_all x0 -> x1, starting transfers between devices: none -> 4.01 us  [per_device(): lax.all_to_all(jnp.stack([query_cluster for _ in range(lax.psum(1, 'split...]
    all_to_all x1, starting transfers between devices: 5.71 us -> 7.17 us  [per_device(): lax.all_to_all(send_cluster.reshape(owners, capacity), 'docs', split_axis...]
    all_to_all x1, starting transfers between devices: 7.17 us -> 5.71 us  [per_device(): lax.all_to_all(send_rank.reshape(owners, capacity), 'docs', split_axis=0,...]
  transfers between devices with their start and end apart: 4 -> 5, of which waited for: 3 -> 3; matrix products, arithmetic and copies ran while one was open for 4% -> 4% of each run, Pallas kernels for 0% -> 0%
where the time goes in v1:
time: 140 us; the launch traced here: 139 us
  blocking collectives  45.5 us (32%)
  waiting for transfers between devices  31.8 us (23%)
  starting transfers between devices  25.2 us (18%)
  between operations  13.6 us (10%)
  local copies, waits for them, and re-layouts  9.8 us (7%)
  other arithmetic  6.98 us (5%)
  matrix products  6.24 us (4%)
    all_to_all x1, blocking collectives, per_device(): lax.all_to_all(send_rows.reshape(owners, capacity, D), 'docs', split_axis...  37.6 us
    all_to_all x1, waiting for transfers between devices, per_device(): lax.all_to_all(top_score.reshape(owners, capacity), 'docs', split_axis=0,...  11.7 us
    all_to_all x1, waiting for transfers between devices, per_device(): lax.all_to_all(send_rank.reshape(owners, capacity), 'docs', split_axis=0,...  10.3 us
    all_to_all x1, waiting for transfers between devices, per_device(): lax.all_to_all(send_cluster.reshape(owners, capacity), 'docs', split_axis...  9.83 us
    all_to_all x1, starting transfers between devices, per_device(): lax.all_to_all(top_score.reshape(owners, capacity), 'docs', split_axis=0,...  8.29 us
    all_gather x1, blocking collectives, per_device(): rank_piece = lax.all_gather(query_rank, 'split', axis=0, tiled=True)  7.91 us
    all_to_all x1, starting transfers between devices, per_device(): lax.all_to_all(send_cluster.reshape(owners, capacity), 'docs', split_axis...  7.17 us
    dot_general x4, matrix products, pair_scores(): jnp.einsum('qd,kd->qk', queries, rows_other, preferred_element_type=jnp.f...  6.24 us
  transfers between devices with their start and end apart: 5, of which 3 were waited for; matrix products, arithmetic and copies ran while one was open for 4% of the time, Pallas kernels for 0%

profile of v1, /device:TPU:1, one launch (start us, length us, event | category | flops | bytes accessed | tf_op | source)
XLA Modules:
  0.0 139.3 jit_solution(9963439865918303955)
XLA Ops:
  6.5 0.0 all-gather.3.cloned.1.call-start
  6.5 0.7 and_select_fusion
  7.2 0.1 fusion.11
  7.3 0.2 reduce_window_sum.11
  7.5 0.2 select_reduce_fusion
  7.6 0.7 compare_select_fusion
  8.3 1.1 fusion.5
  9.4 1.8 %scatter_custom_fusion.2 = bf16[256,1024]{1,0:T(8,128)(2,1)S(1)} fusion(s32[128]{0:T(128)S(1)} %compare_select_fusion, bf16[128,1024]{1,0:T(8,128)(2,1)} %param.5, f32[128]{0:T(128)S(1)} %add_sqrt_fusion, bf16[]{:T(256)} %constant.41.clone.1), kind=kCustom, calls=%fused_computation.17 | custom fusion | flops 393216 | bytes 786946 | tf_op jit(solution)/shard_map/scatter | solution.py:25
  11.2 0.2 reshape.53
  11.4 37.6 %all_to_all.47 = bf16[128,2,1024]{2,1,0:T(2,128)(2,1)S(1)} all-to-all(bf16[128,2,1024]{2,1,0:T(2,128)(2,1)S(1)} %reshape.53), channel_id=1, replica_groups=mesh['docs'=128,'split'=4] {'docs'}, dimensions={0} | all-to-all | bytes 1048576 | tf_op jit(solution)/shard_map/all_to_all | solution.py:29
  49.1 1.0 reshape.54
  50.1 0.0 all-gather.3.cloned.1.call-update
  50.1 1.1 scatter_custom_fusion
  51.2 0.8 all_to_all.31
  51.9 7.2 %all-to-all-start = ((s32[128,1,2]{2,1,0:T(1,128)}), s32[128,1,2]{2,1,0:T(1,128)S(1)}, u32[]{:S(2)}, u32[]{:S(2)}) async-start(s32[128,1,2]{2,1,0:T(1,128)} %bitcast), calls=%async_computation | async-start | bytes 131072 | tf_op jit(solution)/shard_map/all_to_all | solution.py:32
  59.1 1.1 scatter_custom_fusion.1
  60.2 0.8 all_to_all.36
  61.0 9.8 %all-to-all-done = s32[128,1,2]{2,1,0:T(1,128)S(1)} async-done(((s32[128,1,2]{2,1,0:T(1,128)}), s32[128,1,2]{2,1,0:T(1,128)S(1)}, u32[]{:S(2)}, u32[]{:S(2)}) %all-to-all-start) | async-done | bytes 1056 | tf_op jit(solution)/shard_map/all_to_all | solution.py:32
  70.8 0.0 copy-start
  70.8 5.7 %all-to-all-start.2 = ((s32[128,1,2]{2,1,0:T(1,128)}), s32[128,1,2]{2,1,0:T(1,128)S(1)}, u32[]{:S(2)}, u32[]{:S(2)}) async-start(s32[128,1,2]{2,1,0:T(1,128)} %bitcast.2), calls=%async_computation.2 | async-start | bytes 131072 | tf_op jit(solution)/shard_map/all_to_all | solution.py:35
  76.5 0.5 broadcast.50
  77.1 0.7 reduce.9
  77.8 0.1 stack.5
  77.9 10.3 %all-to-all-done.2 = s32[128,1,2]{2,1,0:T(1,128)S(1)} async-done(((s32[128,1,2]{2,1,0:T(1,128)}), s32[128,1,2]{2,1,0:T(1,128)S(1)}, u32[]{:S(2)}, u32[]{:S(2)}) %all-to-all-start.2) | async-done | bytes 1056 | tf_op jit(solution)/shard_map/all_to_all | solution.py:35
  88.2 0.0 copy-start.1
  88.2 0.6 stack.6
  88.8 4.0 %all-to-all-start.1 = ((s32[4,1,256]{2,1,0:T(1,128)}), s32[4,1,256]{2,1,0:T(1,128)S(1)}, u32[]{:S(2)}, u32[]{:S(2)}) async-start(s32[4,1,256]{2,1,0:T(1,128)} %stack.6), calls=%async_computation.1 | async-start | bytes 8192 | tf_op jit(solution)/shard_map/all_to_all | solution.py:56
  92.8 0.7 reduce.10
  93.6 0.1 reshape.93
  93.7 7.9 %all-gather = s32[4,1,256]{2,1,0:T(1,128)S(1)} all-gather(s32[1,1,256]{2,1,0:T(1,128)S(1)} %reshape.93), channel_id=1, replica_groups=mesh['docs'=128,'split'=4] {'split'}, dimensions={0}, use_global_device_ids=true | all-gather | bytes 5120 | tf_op jit(solution)/shard_map/all_gather | solution.py:61
  101.6 0.1 eq.59
  101.8 0.1 lt.37
  101.9 0.0 all-to-all-done.1
  101.9 0.0 all-gather.3.cloned.1.call-done
  102.0 0.0 copy-done
  102.0 0.0 copy-done.1
  102.0 6.5 %while.12 = (s32[]{:T(128)}, f32[256]{0:T(256)S(1)}, s32[128,2]{1,0:T(8,128)}, s32[4,256]{1,0:T(4,128)S(1)}, s32[4,256]{1,0:T(4,128)S(1)}, /*index=5*/s32[128,2]...) while((s32[]{:T(128)}, f32[256]{0:T(256)S(1)}, ...), condition=%wide.wide.region_8.9_spmd.clone, body=%wide.wide.region_6.8_spmd.clone.sunk | while | flops 134545664 | bytes 1061507 | solution.py:73
  102.0 1.6 %fusion.25 = f32[256]{0:T(256)S(1)} fusion(bf16[256,1024]{1,0:T(8,128)(2,1)} %get-tuple-element.222, bf16[4,256,1024]{2,1,0:T(8,128)(2,1)} %get-tuple-element.221, s32[]{:T(128)} %get-tuple-element.203, s32[256]{0:T(256)S(1)} %get-tuple-element.223, s32[256]{0:T(256)S(1)} %get-tuple-element.224, s32[256]{0:T(256)S(1)} %bitcast.43, ...), kind=kOutput, calls=%fused_computation.6.clone.clone.1 | convolution fusion | flops 134545152 | bytes 1054208 | tf_op jit(solution)/shard_map/while/body/eval_jaxpr/qd,kd->qk/dot_general | solution.py:44
  103.6 1.6 %fusion.25 = f32[256]{0:T(256)S(1)} fusion(bf16[256,1024]{1,0:T(8,128)(2,1)} %get-tuple-element.222, bf16[4,256,1024]{2,1,0:T(8,128)(2,1)} %get-tuple-element.221, s32[]{:T(128)} %get-tuple-element.203, s32[256]{0:T(256)S(1)} %get-tuple-element.223, s32[256]{0:T(256)S(1)} %get-tuple-element.224, s32[256]{0:T(256)S(1)} %bitcast.43, ...), kind=kOutput, calls=%fused_computation.6.clone.clone.1 | convolution fusion | flops 134545152 | bytes 1054208 | tf_op jit(solution)/shard_map/while/body/eval_jaxpr/qd,kd->qk/dot_general | solution.py:44
  105.2 1.6 %fusion.25 = f32[256]{0:T(256)S(1)} fusion(bf16[256,1024]{1,0:T(8,128)(2,1)} %get-tuple-element.222, bf16[4,256,1024]{2,1,0:T(8,128)(2,1)} %get-tuple-element.221, s32[]{:T(128)} %get-tuple-element.203, s32[256]{0:T(256)S(1)} %get-tuple-element.223, s32[256]{0:T(256)S(1)} %get-tuple-element.224, s32[256]{0:T(256)S(1)} %bitcast.43, ...), kind=kOutput, calls=%fused_computation.6.clone.clone.1 | convolution fusion | flops 134545152 | bytes 1054208 | tf_op jit(solution)/shard_map/while/body/eval_jaxpr/qd,kd->qk/dot_general | solution.py:44
  106.8 1.6 %fusion.25 = f32[256]{0:T(256)S(1)} fusion(bf16[256,1024]{1,0:T(8,128)(2,1)} %get-tuple-element.222, bf16[4,256,1024]{2,1,0:T(8,128)(2,1)} %get-tuple-element.221, s32[]{:T(128)} %get-tuple-element.203, s32[256]{0:T(256)S(1)} %get-tuple-element.223, s32[256]{0:T(256)S(1)} %get-tuple-element.224, s32[256]{0:T(256)S(1)} %bitcast.43, ...), kind=kOutput, calls=%fused_computation.6.clone.clone.1 | convolution fusion | flops 134545152 | bytes 1054208 | tf_op jit(solution)/shard_map/while/body/eval_jaxpr/qd,kd->qk/dot_general | solution.py:44
  108.4 0.8 all_to_all.40
  109.2 8.3 %all-to-all-start.4 = ((f32[128,1,2]{2,1,0:T(1,128)}), f32[128,1,2]{2,1,0:T(1,128)S(1)}, u32[]{:S(2)}, u32[]{:S(2)}) async-start(f32[128,1,2]{2,1,0:T(1,128)} %bitcast.5), calls=%async_computation.4 | async-start | bytes 131072 | tf_op jit(solution)/shard_map/all_to_all | solution.py:75
  117.5 11.7 %all-to-all-done.4 = f32[128,1,2]{2,1,0:T(1,128)S(1)} async-done(((f32[128,1,2]{2,1,0:T(1,128)}), f32[128,1,2]{2,1,0:T(1,128)S(1)}, u32[]{:S(2)}, u32[]{:S(2)}) %all-to-all-start.4) | async-done | bytes 1056 | tf_op jit(solution)/shard_map/all_to_all | solution.py:75
  129.2 0.5 broadcast.52
  129.7 0.8 reduce.11
  130.5 0.1 reshape.56
  130.7 1.8 %gather_fusion = f32[128]{0:T(128)} fusion(f32[256]{0:T(256)S(1)} %reshape.56, s32[1024]{0:T(1024)S(1)} %pad_clamp_fusion), kind=kCustom, calls=%fused_computation | custom fusion | bytes 1536 | tf_op jit(solution)/shard_map/gather | solution.py:78
  (13 shorter events, 0.1 us)
Async XLA Ops:
  6.5 95.4 %all-gather.3.cloned.1.call-start = ((), (), s32[]{:S(2)}) async-start(), calls=%async_computation.5 | async-start | bytes 2621440 | tf_op jit(solution)/shard_map/all_gather | solution.py:54
  51.9 18.9 %all-to-all-start = ((s32[128,1,2]{2,1,0:T(1,128)}), s32[128,1,2]{2,1,0:T(1,128)S(1)}, u32[]{:S(2)}, u32[]{:S(2)}) async-start(s32[128,1,2]{2,1,0:T(1,128)} %bitcast), calls=%async_computation | async-start | bytes 131072 | tf_op jit(solution)/shard_map/all_to_all | solution.py:32
  70.8 31.1 %copy-start = (s32[128,1,2]{2,1,0:T(1,128)}, s32[128,1,2]{2,1,0:T(1,128)S(1)}, u32[]{:S(2)}) copy-start(s32[128,1,2]{2,1,0:T(1,128)S(1)} %all-to-all-done) | copy-start | bytes 3076
  70.8 17.4 %all-to-all-start.2 = ((s32[128,1,2]{2,1,0:T(1,128)}), s32[128,1,2]{2,1,0:T(1,128)S(1)}, u32[]{:S(2)}, u32[]{:S(2)}) async-start(s32[128,1,2]{2,1,0:T(1,128)} %bitcast.2), calls=%async_computation.2 | async-start | bytes 131072 | tf_op jit(solution)/shard_map/all_to_all | solution.py:35
  88.2 13.8 %copy-start.1 = (s32[128,1,2]{2,1,0:T(1,128)}, s32[128,1,2]{2,1,0:T(1,128)S(1)}, u32[]{:S(2)}) copy-start(s32[128,1,2]{2,1,0:T(1,128)S(1)} %all-to-all-done.2) | copy-start | bytes 3076
  88.8 13.1 %all-to-all-start.1 = ((s32[4,1,256]{2,1,0:T(1,128)}), s32[4,1,256]{2,1,0:T(1,128)S(1)}, u32[]{:S(2)}, u32[]{:S(2)}) async-start(s32[4,1,256]{2,1,0:T(1,128)} %stack.6), calls=%async_computation.1 | async-start | bytes 8192 | tf_op jit(solution)/shard_map/all_to_all | solution.py:56
  109.2 20.0 %all-to-all-start.4 = ((f32[128,1,2]{2,1,0:T(1,128)}), f32[128,1,2]{2,1,0:T(1,128)S(1)}, u32[]{:S(2)}, u32[]{:S(2)}) async-start(f32[128,1,2]{2,1,0:T(1,128)} %bitcast.5), calls=%async_computation.4 | async-start | bytes 131072 | tf_op jit(solution)/shard_map/all_to_all | solution.py:75
Sparse Core Ops, SparseCore 0:
  50.2 29.5 all-gather.2
